TPU v7x, 32 devices: a whole 2x2x4 slice. The times are simulated.
32 devices in a mesh: dp: 8 (over z, x), shard: 4 (over y, core).
Axes of the slice: x: 2, y: 2, z: 4, core: 2. Of those that a mesh axis runs over, the one named last changes fastest.
Arguments:
- grads: bfloat16 [8, 384, 8192], P('dp', 'shard'), may hold values from -6 to 6
- momentum: float32 [8, 384, 8192], P('dp', 'shard'), may hold values from -6 to 6
- param: float32 [384, 8192], P('shard'), may hold values from -6 to 6
- thresholds: float32 [384], P('shard'), may hold values from 0.1 to 1
- sel_blocks: int32 [8, 4, 768], P(None, 'shard'), may hold values from 0 to 6143, as said below
- counts: int32 [8, 4], P(None, 'shard'), may hold values from 192 to 768, as said below
Outputs:
- new_momentum: float32 [8, 384, 8192], P('dp', 'shard')
- new_param: float32 [384, 8192], P('shard')
- compute_copy: bfloat16 [384, 8192], replicated
Inputs may be any that keep to these rules, and one draw needn't show every extreme that they name: `sel_blocks`: within one replica and shard the 768 entries are distinct block numbers of that shard. `counts`: some replica has 768 live slots in every shard.
All inputs are finite; a program needn't handle non-finite values.
Results may differ from a plain program's by a relative error of at most 0.0019.
Values may be sent and summed in bfloat16 or wider, within the bound.
A program may use at most 128 MiB of HBM per device.

v0:
```python
import math

import jax
import jax.numpy as jnp
from jax import lax
from jax.sharding import PartitionSpec as P

D = 8192
KMAX = 768


beta_decay = 0.999
step_size = 0.1


def dct_table():
    positions = jnp.arange(128, dtype=jnp.int32)
    sample = (positions % 64)[:, None]
    freq = (positions % 64)[None, :]
    same_half = positions[:, None] // 64 == positions[None, :] // 64
    weights = jnp.where(freq == 0, math.sqrt(1.0 / 64.0), math.sqrt(2.0 / 64.0)).astype(jnp.float32)
    angles = ((2 * sample + 1) * freq).astype(jnp.float32) * (math.pi / 128.0)
    return jnp.where(same_half, weights * jnp.cos(angles), 0.0)


def on_device(grads, momentum, param, thresholds, sel_blocks, counts):
    table = dct_table()
    per_row = D // 128
    replica = lax.axis_index("dp")
    blended = beta_decay * momentum[0] + grads[0].astype(jnp.float32)
    coefficients = jnp.dot(
        blended.reshape(-1, 128),
        table,
        precision=lax.Precision.HIGHEST,
        preferred_element_type=jnp.float32,
    )
    thr_blocks = jnp.repeat(thresholds, per_row)[:, None]
    shrunk = coefficients - jnp.clip(coefficients, -thr_blocks, thr_blocks)
    sel_local = sel_blocks[:, 0, :]
    own_ids = lax.dynamic_index_in_dim(sel_local, replica, 0, keepdims=False)
    own_count = lax.dynamic_index_in_dim(counts[:, 0], replica, 0, keepdims=False)
    live_slots = jnp.arange(KMAX, dtype=jnp.int32) < own_count
    sent = jnp.where(live_slots[:, None], shrunk[own_ids], 0.0).astype(jnp.bfloat16)
    widened = lax.optimization_barrier(sent).astype(jnp.float32)
    own_dense = jnp.zeros_like(coefficients).at[own_ids].add(widened)
    decoded = jnp.dot(
        own_dense, table.T, precision=lax.Precision.HIGHEST, preferred_element_type=jnp.float32
    )
    new_momentum = blended - decoded.reshape(blended.shape)
    piece_ids = sel_local.reshape(-1)
    total = (
        jnp.zeros_like(coefficients)
        .at[piece_ids]
        .add(
            lax.all_gather(sent[None], "dp", axis=0, tiled=True)
            .reshape(-1, 128)
            .astype(jnp.float32)
        )
    )
    averaged = total / lax.axis_size("dp")
    direction = jnp.dot(
        averaged, table.T, precision=lax.Precision.HIGHEST, preferred_element_type=jnp.float32
    ).reshape(param.shape)
    update = jnp.tanh(
        direction * lax.rsqrt(jnp.mean(direction * direction, axis=1, keepdims=True) + 1e-06)
    )
    new_param = param - step_size * update
    compute_copy = lax.all_gather(new_param.astype(jnp.bfloat16), "shard", axis=0, tiled=True)
    return (new_momentum[None], new_param, compute_copy)


def solution(mesh):
    placed = (
        P("dp", "shard", None),
        P("dp", "shard", None),
        P("shard", None),
        P("shard"),
        P(None, "shard", None),
        P(None, "shard"),
    )
    return jax.shard_map(
        on_device,
        mesh=mesh,
        in_specs=placed,
        out_specs=(P("dp", "shard", None), P("shard", None), P()),
        check_vma=False,
    )
```

profile of v0, /device:TPU:0, one launch (start us, length us, event | category | flops | bytes accessed | tf_op | source)
XLA Modules:
  0.0 186.9 jit_solution(2573512832816448879)
XLA Ops:
  7.2 0.0 copy-start
  7.2 0.0 all-gather.3.cloned.1.call-start
  7.3 0.0 copy-start.2
  7.3 0.0 copy-start.3
  7.3 0.5 copy-done
  7.8 0.6 constant_dynamic-slice_fusion
  8.4 0.6 iota_compare_fusion
  9.1 0.0 copy-start.4
  9.1 0.7 fusion.36
  9.8 0.7 broadcast_in_dim.46
  10.5 0.1 min.14
  10.6 2.7 %convert_add_fusion = f32[1,96,8192]{2,1,0:T(8,128)S(1)} fusion(bf16[1,96,8192]{2,1,0:T(8,128)(2,1)} %param.6, f32[1,96,8192]{2,1,0:T(8,128)} %param.7), kind=kLoop, calls=%fused_computation.10 | loop fusion | flops 2359296 | bytes 7864320 | tf_op jit(solution)/shard_map/add | solution.py:30
  13.3 2.3 %add.104 = f32[6144,128]{1,0:T(8,128)} reshape(f32[1,96,8192]{2,1,0:T(8,128)S(1)} %convert_add_fusion) | data formatting | bytes 6291456 | tf_op jit(solution)/shard_map/add | solution.py:30
  15.6 0.0 copy-start.1
  15.6 5.7 %minimum_subtract_fusion = bf16[6144,128]{1,0:T(8,128)(2,1)} fusion(f32[6144]{0:T(1024)S(1)} %neg.8, f32[6144]{0:T(1024)S(1)} %min.14, f32[6144,128]{1,0:T(8,128)} %add.104, s32[128]{0:T(128)S(1)} %get-tuple-element.7, s32[128]{0:T(128)S(1)} %multiply_add_fusion, f32[128]{0:T(128)S(1)} %compare_select_fusion.2, s32[128]{0:T(128)S(1)} %get-tuple-element.8), kind=kOutput, calls=%fused_computation.9 | convolution fusion | flops 1211203584 | bytes 4769792 | tf_op jit(solution)/shard_map/dot_general | solution.py:31
  21.3 3.2 %gather_fusion = bf16[768,128]{1,0:T(8,128)(2,1)S(1)} fusion(bf16[6144,128]{1,0:T(8,128)(2,1)} %minimum_subtract_fusion, s32[1024]{0:T(1024)S(1)} %pad_clamp_fusion), kind=kCustom, calls=%fused_computation | custom fusion | bytes 396288 | tf_op jit(solution)/shard_map/gather | solution.py:43
  24.6 0.0 copy-done.4
  24.6 0.8 fusion.8
  25.4 0.0 all-gather.3.cloned.1.call-update
  25.4 0.0 all-gather.5.cloned.1.call-start
  25.5 0.0 copy-done.1
  25.5 47.0 %all-gather.3.cloned.1.call-done = bf16[8,768,128]{2,1,0:T(8,128)(2,1)} async-done(((bf16[1,768,128]{2,1,0:T(8,128)(2,1)}), bf16[8,768,128]{2,1,0:T(8,128)(2,1)}) %all-gather.3.cloned.1.call-update) | async-done | bytes 1572880 | tf_op jit(solution)/shard_map/all_gather | solution.py:55
  72.5 35.5 %scatter_custom_fusion.1 = f32[6144,128]{1,0:T(8,128)} fusion(s32[6144]{0:T(1024)S(1)} %bitcast.15, bf16[6144,128]{1,0:T(8,128)(2,1)} %bitcast.13, f32[]{:T(128)} %constant.76.clone.1), kind=kCustom, calls=%fused_computation.3 | custom fusion | flops 1572864 | bytes 4718596 | tf_op jit(solution)/shard_map/scatter-add | solution.py:54
  108.0 0.0 copy-done.2
  108.0 0.0 copy-done.3
  108.0 7.0 %multiply_reduce_fusion = (f32[6144]{0:T(1024)S(1)}, f32[6144,128]{0,1:T(8,128)}) fusion(s32[128]{0:T(128)S(1)} %get-tuple-element.7, s32[128]{0:T(128)S(1)} %multiply_add_fusion, f32[128]{0:T(128)S(1)} %compare_select_fusion.2, s32[128]{0:T(128)S(1)} %get-tuple-element.8, f32[6144,128]{1,0:T(8,128)} %scatter_custom_fusion.1), kind=kOutput, calls=%fused_computation.6 | convolution fusion | flops 1210411008 | bytes 6318080 | tf_op jit(solution)/shard_map/dot_general | solution.py:61
  115.0 0.1 reduce_sum.14
  115.1 0.1 reduce_sum.18
  115.2 3.6 %copy.10 = f32[6144,128]{1,0:T(8,128)} copy(f32[6144,128]{0,1:T(8,128)} %get-tuple-element.6) | data formatting | bytes 6291456 | tf_op jit(solution)/shard_map/dot_general | solution.py:61
  118.8 4.6 %reshape.236 = f32[96,8192]{1,0:T(8,128)} reshape(f32[6144,128]{1,0:T(8,128)} %copy.10) | data formatting | bytes 6291456 | tf_op jit(solution)/shard_map/reshape | solution.py:63
  123.4 5.6 %fusion.44 = (bf16[96,8192]{1,0:T(8,128)(2,1)}, f32[96,8192]{1,0:T(8,128)}) fusion(f32[96,8192]{1,0:T(8,128)} %param.8, f32[96,8192]{1,0:T(8,128)} %reshape.236, f32[96]{0:T(128)S(1)} %add_rsqrt_fusion), kind=kLoop, calls=%fused_computation.67 | loop fusion | flops 3145728 | bytes 11010432 | tf_op jit(solution)/shard_map/convert_element_type | solution.py:68
  129.0 0.0 all-gather.5.cloned.1.call-update
  129.0 0.9 select_convert_fusion
  129.8 7.6 %scatter_custom_fusion = f32[6144,128]{1,0:T(8,128)} fusion(s32[768]{0:T(1024)S(1)} %fusion.36, f32[]{:T(128)} %constant.76.clone.1, bf16[768,128]{1,0:T(8,128)(2,1)S(1)} %select_convert_fusion), kind=kCustom, calls=%fused_computation.13 | custom fusion | flops 196608 | bytes 3342340 | tf_op jit(solution)/shard_map/scatter-add | solution.py:45
  137.4 6.3 %fusion.10 = f32[6144,128]{1,0:T(8,128)} fusion(f32[6144,128]{1,0:T(8,128)} %scatter_custom_fusion, s32[128]{0:T(128)} %copy-done.3, s32[128]{0:T(128)S(1)} %multiply_add_fusion, f32[128]{0:T(128)} %copy-done.2, s32[128]{0:T(128)S(1)} %get-tuple-element.8), kind=kOutput, calls=%fused_computation.21 | convolution fusion | flops 1208057856 | bytes 6293504 | tf_op jit(solution)/shard_map/dot_general | solution.py:46
  143.7 4.6 %reshape.235 = f32[1,96,8192]{2,1,0:T(8,128)} reshape(f32[6144,128]{1,0:T(8,128)} %fusion.10) | data formatting | bytes 6291456 | tf_op jit(solution)/shard_map/reshape | solution.py:49
  148.3 4.1 %sub.26 = f32[1,96,8192]{2,1,0:T(8,128)} subtract(f32[1,96,8192]{2,1,0:T(8,128)S(1)} %convert_add_fusion, f32[1,96,8192]{2,1,0:T(8,128)} %reshape.235) | non-fusion elementwise | flops 786432 | bytes 9437184 | tf_op jit(solution)/shard_map/sub | solution.py:49
  152.4 21.5 %all-gather.5.cloned.1.call-done = bf16[384,8192]{1,0:T(8,128)(2,1)} async-done(((bf16[96,8192]{1,0:T(8,128)(2,1)}), bf16[384,8192]{1,0:T(8,128)(2,1)}) %all-gather.5.cloned.1.call-update) | async-done | bytes 6291472 | tf_op jit(solution)/shard_map/all_gather | solution.py:68
  173.9 6.2 %copy.12 = bf16[384,8192]{1,0:T(8,128)(2,1)} copy(bf16[384,8192]{1,0:T(8,128)(2,1)} %all-gather.5.cloned.1.call-done) | data formatting | bytes 12582912
  (7 shorter events, 0.1 us)
Async XLA Ops:
  7.2 0.7 copy-start
  7.2 65.3 %all-gather.3.cloned.1.call-start = ((), (), s32[]{:S(2)}) async-start(), calls=%async_computation | async-start | bytes 1769472 | tf_op jit(solution)/shard_map/all_gather | solution.py:55
  7.3 100.7 %copy-start.2 = (f32[128]{0:T(128)}, f32[128]{0:T(128)S(1)}, u32[]{:S(2)}) copy-start(f32[128]{0:T(128)S(1)} %compare_select_fusion.2) | copy-start | bytes 1540
  7.3 100.7 %copy-start.3 = (s32[128]{0:T(128)}, s32[128]{0:T(128)S(1)}, u32[]{:S(2)}) copy-start(s32[128]{0:T(128)S(1)} %get-tuple-element.7) | copy-start | bytes 1540
  9.1 15.5 %copy-start.4 = (pred[768]{0:T(1024)(128)(4,1)}, pred[768]{0:T(1024)(128)(4,1)S(1)}, u32[]{:S(2)}) copy-start(pred[768]{0:T(1024)(128)(4,1)S(1)} %iota_compare_fusion) | copy-start | bytes 2308
  15.6 9.9 %copy-start.1 = (s32[8,1,768]{2,1,0:T(1,128)S(1)}, s32[8,1,768]{2,1,0:T(1,128)}, u32[]{:S(2)}) copy-start(s32[8,1,768]{2,1,0:T(1,128)} %param.10) | copy-start | bytes 73732
  25.4 148.4 %all-gather.5.cloned.1.call-start = ((), (), s32[]{:S(2)}) async-start(), calls=%async_computation.1 | async-start | bytes 7864320 | tf_op jit(solution)/shard_map/all_gather | solution.py:68
Sparse Core Ops, SparseCore 0:
  25.6 46.8 all-gather.2
  129.1 44.7 all-gather.4
where the time goes:
time: 187 us
  waiting for transfers between devices  68.5 us (37%)
  other arithmetic  58.7 us (31%)
  local copies, waits for them, and re-layouts  26.4 us (14%)
  matrix products  19.1 us (10%)
  between operations  14.2 us (8%)
    all_gather x1, waiting for transfers between devices, on_device(): lax.all_gather(sent[None], 'dp', axis=0, tiled=True).reshape(-1, 128)  47 us
    scatter-add x1, other arithmetic, on_device(): total = jnp.zeros_like(coefficients).at[piece_ids].add(lax.all_gather(sen...  35.5 us
    all_gather x1, waiting for transfers between devices, on_device(): lax.all_gather(new_param.astype(jnp.bfloat16), 'shard', axis=0, tiled=True)  21.5 us
    scatter-add x1, other arithmetic, on_device(): own_dense = jnp.zeros_like(coefficients).at[own_ids].add(widened)  7.57 us
    dot_general x1, matrix products, on_device(): jnp.dot(averaged, table.T, precision=lax.Precision.HIGHEST, preferred_ele...  7.04 us
    unnamed x11, local copies, waits for them, and re-layouts  6.76 us
    dot_general x1, matrix products, on_device(): jnp.dot(own_dense, table.T, precision=lax.Precision.HIGHEST, preferred_el...  6.29 us
    dot_general x1, matrix products, on_device(): jnp.dot(blended.reshape(-1, 128), table, precision=lax.Precision.HIGHEST,...  5.72 us
  transfers between devices with their start and end apart: 2, of which 2 were waited for; matrix products, arithmetic and copies ran while one was open for 13% of the time, Pallas kernels for 0%

commit v1 on v0

v1 whole, which is shorter than its diff:
```python
import functools

import jax
import jax.numpy as jnp
import numpy as np
from jax import lax
from jax.experimental import pallas as pl
from jax.experimental.pallas import tpu as pltpu
from jax.sharding import PartitionSpec as P

BLK = 128
HALF = 64
beta_decay = 0.999
step_size = 0.1
UNROLL = 16


def tables():
    pos = np.arange(BLK)
    sample, freq = (pos % HALF)[:, None], (pos % HALF)[None, :]
    same = pos[:, None] // HALF == pos[None, :] // HALF
    weights = np.where(freq == 0, np.sqrt(1.0 / HALF), np.sqrt(2.0 / HALF))
    table = np.where(same, weights * np.cos((2 * sample + 1) * freq * (np.pi / BLK)), 0.0).astype(np.float32)

    def wide(t):
        hi = t.astype(jnp.bfloat16)
        lo = (t - hi.astype(np.float32)).astype(jnp.bfloat16)
        half = np.concatenate([hi, lo], axis=1)
        return np.concatenate([half, half], axis=0)

    return wide(table), wide(table.T)


def split(x):
    hi = x.astype(jnp.bfloat16)
    lo = (x - hi.astype(jnp.float32)).astype(jnp.bfloat16)
    return jnp.concatenate([hi, lo], axis=1)


def both(x, w):
    y = jnp.dot(x, w, preferred_element_type=jnp.float32)
    return y[:, :BLK] + y[:, BLK:]


def tiles(x):
    return jnp.concatenate([x[:, c * BLK : (c + 1) * BLK] for c in range(x.shape[1] // BLK)], axis=0)


def encode_kernel(per_row, mom, grad, thr, sel, place, counts, fwd, inv, newmom, sent, rowhot, dense, picked):
    step = pl.program_id(0)
    replica = lax.axis_index("dp")
    rows, width = mom.shape
    slots = sel.shape[1]
    cols = width // BLK
    ids = sel[pl.ds(replica, 1), :]

    @pl.when(step == 0)
    def _():
        live = lax.broadcasted_iota(jnp.int32, (1, slots), 1) < counts[replica, 0]
        row_of = jnp.where(live, ids // per_row, -1)
        hot = row_of == lax.broadcasted_iota(jnp.int32, (rows, slots), 0)
        rowhot[...] = jnp.where(hot, 1.0, 0.0).astype(jnp.bfloat16)

    colhot = ids % per_row == step * cols + lax.broadcasted_iota(jnp.int32, (max(cols, 8), slots), 0)
    mask = lax.dot_general(
        rowhot[...],
        jnp.where(colhot, 1.0, 0.0).astype(jnp.bfloat16),
        (((1,), (1,)), ((), ())),
        preferred_element_type=jnp.float32,
    )
    blended = tiles(beta_decay * mom[...] + grad[...].astype(jnp.float32))
    coef = both(split(blended), fwd[...])
    t = jnp.concatenate([jnp.broadcast_to(thr[...], (rows, BLK))] * cols, axis=0)
    shrunk = coef - jnp.clip(coef, -t, t)
    keep = jnp.concatenate([jnp.broadcast_to(mask[:, c : c + 1], (rows, BLK)) for c in range(cols)], axis=0)
    kept = jnp.where(keep > 0.5, shrunk, 0.0)
    dense[pl.ds(pl.multiple_of(step * (cols * rows), 8), cols * rows), :] = kept
    out = blended - both(kept.astype(jnp.bfloat16), inv[:BLK, :])
    for c in range(cols):
        newmom[:, c * BLK : (c + 1) * BLK] = out[c * rows : (c + 1) * rows]

    @pl.when(step == pl.num_programs(0) - 1)
    def _():
        def pick(i, carry):
            base = i * UNROLL
            got = [dense[pl.ds(place[replica, base + u], 1), :] for u in range(UNROLL)]
            for u in range(UNROLL):
                picked[pl.ds(base + u, 1), :] = got[u]
            return carry

        lax.fori_loop(0, slots // UNROLL, pick, 0)
        sent[...] = picked[...].astype(jnp.bfloat16)


def encode(mom, grad, thr, sel, place, counts, fwd, inv, width):
    rows, D = mom.shape
    reps, slots = sel.shape
    col = pl.BlockSpec((rows, width), lambda i: (0, i))
    whole = lambda a: pl.BlockSpec(a.shape, lambda i: (0,) * a.ndim)
    smem = pl.BlockSpec(memory_space=pltpu.SMEM)
    return pl.pallas_call(
        functools.partial(encode_kernel, D // BLK),
        grid=(D // width,),
        in_specs=[col, col, whole(thr), whole(sel), smem, smem, whole(fwd), whole(inv)],
        out_specs=[col, pl.BlockSpec((slots, BLK), lambda i: (0, 0))],
        out_shape=[
            jax.ShapeDtypeStruct(mom.shape, jnp.float32),
            jax.ShapeDtypeStruct((slots, BLK), jnp.bfloat16),
        ],
        scratch_shapes=[
            pltpu.VMEM((rows, slots), jnp.bfloat16),
            pltpu.VMEM((rows * (D // BLK), BLK), jnp.float32),
            pltpu.VMEM((slots, BLK), jnp.float32),
        ],
        name="encode",
    )(mom, grad, thr, sel, place, counts, fwd, inv)


def apply_kernel(reps, place, sent, param, inv, newparam, copy, total, wide, scale):
    step = pl.program_id(0)
    rows, width = param.shape
    slots = wide.shape[0]
    cols = width // BLK
    all_cols = total.shape[0] // rows

    @pl.when(step == 0)
    def _():
        total[...] = jnp.zeros_like(total)

    @pl.when(step < reps)
    def _():
        wide[...] = sent[0].astype(jnp.float32)

        def put(i, carry):
            base = pl.multiple_of(i * UNROLL, UNROLL)
            at = [place[step, base + u] for u in range(UNROLL)]
            new = [total[pl.ds(at[u], 1), :] + wide[pl.ds(base + u, 1), :] for u in range(UNROLL)]
            for u in range(UNROLL):
                total[pl.ds(at[u], 1), :] = new[u]
            return carry

        lax.fori_loop(0, slots // UNROLL, put, 0)

    @pl.when(step == reps)
    def _():
        def square(c, acc):
            a = total[pl.ds(pl.multiple_of(c * rows, 8), rows), :] * (1.0 / reps)
            return acc + a * a

        acc = lax.fori_loop(0, all_cols, square, jnp.zeros((rows, BLK), jnp.float32), unroll=4)
        mean = jnp.sum(acc, axis=1, keepdims=True) * (1.0 / (all_cols * BLK))
        scale[...] = jnp.broadcast_to(lax.rsqrt(mean + 1e-06), scale.shape)

    @pl.when(step >= reps)
    def _():
        at = pl.multiple_of((step - reps) * (cols * rows), 8)
        averaged = total[pl.ds(at, cols * rows), :] * (1.0 / reps)
        direction = both(split(averaged), inv[...])
        for c in range(cols):
            lanes = slice(c * BLK, (c + 1) * BLK)
            update = jnp.tanh(direction[c * rows : (c + 1) * rows] * scale[...])
            new = param[:, lanes] - step_size * update
            newparam[:, lanes] = new
            copy[:, lanes] = new.astype(jnp.bfloat16)


def apply(place, sent, param, inv, width):
    rows, D = param.shape
    reps, slots, _ = sent.shape
    col = pl.BlockSpec((rows, width), lambda i: (0, jnp.maximum(i - reps, 0)))
    return pl.pallas_call(
        functools.partial(apply_kernel, reps),
        grid=(reps + D // width,),
        in_specs=[
            pl.BlockSpec(memory_space=pltpu.SMEM),
            pl.BlockSpec((1, slots, BLK), lambda i: (jnp.minimum(i, reps - 1), 0, 0)),
            col,
            pl.BlockSpec(inv.shape, lambda i: (0, 0)),
        ],
        out_specs=[col, col],
        out_shape=[
            jax.ShapeDtypeStruct(param.shape, jnp.float32),
            jax.ShapeDtypeStruct(param.shape, jnp.bfloat16),
        ],
        scratch_shapes=[
            pltpu.VMEM((rows * (D // BLK), BLK), jnp.float32),
            pltpu.VMEM((slots, BLK), jnp.float32),
            pltpu.VMEM((rows, BLK), jnp.float32),
        ],
        name="apply",
    )(place, sent, param, inv)


def on_device(grads, momentum, param, thresholds, sel_blocks, counts):
    rows, D = param.shape
    per_row = D // BLK
    width = min(1024, D)
    fwd, inv = (jnp.asarray(t) for t in tables())
    sel = sel_blocks[:, 0, :]
    place = (sel % per_row) * rows + sel // per_row
    new_momentum, sent = encode(
        momentum[0], grads[0], thresholds[:, None], sel, place, counts, fwd, inv, width
    )
    gathered = lax.all_gather(sent, "dp", axis=0, tiled=False)
    new_param, copy = apply(place, gathered, param, inv, width)
    compute_copy = lax.all_gather(copy, "shard", axis=0, tiled=True)
    return (new_momentum[None], new_param, compute_copy)


def solution(mesh):
    placed = (
        P("dp", "shard", None),
        P("dp", "shard", None),
        P("shard", None),
        P("shard"),
        P(None, "shard", None),
        P(None, "shard"),
    )
    return jax.shard_map(
        on_device,
        mesh=mesh,
        in_specs=placed,
        out_specs=(P("dp", "shard", None), P("shard", None), P()),
        check_vma=False,
    )
```

time: 187 us -> 161 us (0.86)
  other arithmetic: 58.7 us -> 1.36 us
  Pallas kernels: 0 us -> 42.7 us
  waiting for transfers between devices: 68.5 us -> 91.9 us
  matrix products: 19.1 us -> 0 us
  local copies, waits for them, and re-layouts: 26.4 us -> 10.2 us
    scatter-add x2 -> x0, other arithmetic: 43 us -> none  [the longest x1 35.5 us: on_device(): total = jnp.zeros_like(coefficients).at[piece_ids].add(lax.all_gather(sen...]
    pallas_call x0 -> x2, Pallas kernels: none -> 42.7 us  [the longest x1 31.8 us: apply(): pl.pallas_call(functools.partial(apply_kernel, reps), grid=(reps + D // w...]
    all_gather x2, waiting for transfers between devices: 68.4 us -> 91.9 us  [the longest x1 47 us: on_device(): gathered = lax.all_gather(sent, 'dp', axis=0, tiled=False)]
    dot_general x3 -> x0, matrix products: 19.1 us -> none  [the longest x1 7.04 us: on_device(): jnp.dot(averaged, table.T, precision=lax.Precision.HIGHEST, preferred_ele...]
    reshape x2 -> x0, local copies, waits for them, and re-layouts: 9.18 us -> none  [the longest x1 4.59 us: on_device(): direction = jnp.dot(averaged, table.T, precision=lax.Precision.HIGHEST, p...]
    convert_element_type x3 -> x0, other arithmetic: 7.31 us -> none  [the longest x1 5.61 us: on_device(): new_param.astype(jnp.bfloat16)]
    sub x1 -> x0, other arithmetic: 4.11 us -> none  [on_device(): new_momentum = blended - decoded.reshape(blended.shape)]
    dot_general x1 -> x0, local copies, waits for them, and re-layouts: 3.55 us -> none  [on_device(): jnp.dot(averaged, table.T, precision=lax.Precision.HIGHEST, preferred_ele...]
  transfers between devices with their start and end apart: 2 -> 2, of which waited for: 2 -> 2; matrix products, arithmetic and copies ran while one was open for 13% -> 0% of each run, Pallas kernels for 0% -> 0%
where the time goes in v1:
time: 161 us; the launch traced here: 160 us
  waiting for transfers between devices  91.9 us (57%)
  Pallas kernels  42.7 us (27%)
  between operations  14 us (9%)
  local copies, waits for them, and re-layouts  10.2 us (6%)
    all_gather x1, waiting for transfers between devices, on_device(): gathered = lax.all_gather(sent, 'dp', axis=0, tiled=False)  47 us
    all_gather x1, waiting for transfers between devices, on_device(): compute_copy = lax.all_gather(copy, 'shard', axis=0, tiled=True)  44.9 us
    pallas_call x1, Pallas kernels, apply(): pl.pallas_call(functools.partial(apply_kernel, reps), grid=(reps + D // w...  31.8 us
    pallas_call x1, Pallas kernels, encode(): pl.pallas_call(functools.partial(encode_kernel, D // BLK), grid=(D // wid...  10.9 us
    unnamed x3, local copies, waits for them, and re-layouts  8.85 us
  transfers between devices with their start and end apart: 2, of which 2 were waited for; matrix products, arithmetic and copies ran while one was open for 0% of the time, Pallas kernels for 0%

profile of v1, /device:TPU:0, one launch (start us, length us, event | category | flops | bytes accessed | tf_op | source)
XLA Modules:
  0.0 160.3 jit_solution(15838795051071735357)
XLA Ops:
  7.2 0.0 all-gather.6.cloned.1.call-start
  7.2 1.4 fusion.1.place
  8.6 1.3 copy.17
  9.9 1.3 copy.12.counts
  11.2 1.4 copy.11.thr
  12.6 10.9 %encode.1 = (f32[96,8192]{1,0:T(8,128)}, bf16[768,128]{1,0:T(8,128)(2,1)}) custom-call(f32[96,8192]{1,0:T(8,128)} %bitcast.10, bf16[96,8192]{1,0:T(8,128)(2,1)} %bitcast.11, f32[96,1]{1,0:T(8,128)} %copy.11.thr, s32[8,768]{1,0:T(8,128)} %bitcast.13, s32[8,768]{1,0:T(8,128)} %fusion.1.place, s32[8,1]{1,0:T(8,128)} %copy.12.counts, ...), custom_call_target="tpu_custom_call" | custom-call | tf_op jit(solution)/shard_map/encode/pallas_call | solution.py:101
  23.5 0.0 all-gather.6.cloned.1.call-update
  23.5 0.0 all-gather.4.cloned.1.call-start
  23.6 47.0 %all-gather.6.cloned.1.call-done = bf16[6144,128]{1,0:T(8,128)(2,1)} async-done(((bf16[768,128]{1,0:T(8,128)(2,1)}), bf16[6144,128]{1,0:T(8,128)(2,1)}) %all-gather.6.cloned.1.call-update) | async-done | bytes 1572880 | tf_op jit(solution)/shard_map/all_gather | solution.py:204
  70.6 31.8 %apply.1 = (f32[96,8192]{1,0:T(8,128)}, bf16[96,8192]{1,0:T(8,128)(2,1)}) custom-call(s32[8,768]{1,0:T(8,128)} %fusion.1.place, bf16[8,768,128]{2,1,0:T(8,128)(2,1)} %bitcast.12, f32[96,8192]{1,0:T(8,128)} %param.15, bf16[256,256]{1,0:T(8,128)(2,1)} %constant.35.clone.inv), custom_call_target="tpu_custom_call" | custom-call | tf_op jit(solution)/shard_map/apply/pallas_call | solution.py:171
  102.4 0.0 all-gather.4.cloned.1.call-update
  102.4 44.9 %all-gather.4.cloned.1.call-done = bf16[384,8192]{1,0:T(8,128)(2,1)} async-done(((bf16[96,8192]{1,0:T(8,128)(2,1)}), bf16[384,8192]{1,0:T(8,128)(2,1)}) %all-gather.4.cloned.1.call-update) | async-done | bytes 6291472 | tf_op jit(solution)/shard_map/all_gather | solution.py:206
  147.3 6.2 %copy.19 = bf16[384,8192]{1,0:T(8,128)(2,1)} copy(bf16[384,8192]{1,0:T(8,128)(2,1)} %all-gather.4.cloned.1.call-done) | data formatting | bytes 12582912
Async XLA Ops:
  7.2 63.4 %all-gather.6.cloned.1.call-start = ((), (), s32[]{:S(2)}) async-start(), calls=%async_computation.1 | async-start | bytes 1769472 | tf_op jit(solution)/shard_map/all_gather | solution.py:204
  23.5 123.8 %all-gather.4.cloned.1.call-start = ((), (), s32[]{:S(2)}) async-start(), calls=%async_computation | async-start | bytes 7864320 | tf_op jit(solution)/shard_map/all_gather | solution.py:206
Sparse Core Ops, SparseCore 0:
  23.7 46.8 all-gather.5
  102.5 44.7 all-gather.3

commit v2 on v1

--- a/solution.py
+++ b/solution.py
@@ -191,6 +191,195 @@
     )(place, sent, param, inv)
 
 
+MESH = pl.DeviceIdType.MESH
+
+
+def copy_to(src, dst, send, recv, peer):
+    return pltpu.make_async_remote_copy(
+        src_ref=src, dst_ref=dst, send_sem=send, recv_sem=recv, device_id=peer, device_id_type=MESH
+    )
+
+
+def share_sent_kernel(reps, mine, out, send, recv, local):
+    me = lax.axis_index("dp")
+    line, side = me // 2, lax.rem(me, 2)
+    length = reps // 2
+    up, down, across = {"dp": me + 2}, {"dp": me - 2}, {"dp": me + 1 - 2 * side}
+    has_up, has_down = line < length - 1, line > 0
+
+    barrier = pltpu.get_barrier_semaphore()
+    pl.semaphore_signal(barrier, inc=1, device_id=across, device_id_type=MESH)
+
+    @pl.when(has_up)
+    def _():
+        pl.semaphore_signal(barrier, inc=1, device_id=up, device_id_type=MESH)
+
+    @pl.when(has_down)
+    def _():
+        pl.semaphore_signal(barrier, inc=1, device_id=down, device_id_type=MESH)
+
+    pl.semaphore_wait(barrier, 1 + jnp.where(has_up, 1, 0) + jnp.where(has_down, 1, 0))
+
+    def block(i, way, peer, own=False):
+        src = mine if own else out.at[i]
+        return copy_to(src, out.at[i], send.at[i, way], recv.at[i], peer)
+
+    for act in ("start", "wait_send"):
+        begin = act == "start"
+        if begin:
+            keep = pltpu.make_async_copy(mine, out.at[me], local)
+            keep.start()
+
+        @pl.when(has_up)
+        def _():
+            getattr(block(me, 0, up, True), act)()
+
+        @pl.when(has_down)
+        def _():
+            getattr(block(me, 1, down, True), act)()
+
+        getattr(block(me, 2, across, True), act)()
+        for d in range(1, length):
+
+            @pl.when(line >= d)
+            def _():
+                i = me - 2 * d
+                if begin:
+                    block(i, 0, across).wait_recv()
+
+                @pl.when(has_up)
+                def _():
+                    getattr(block(i, 0, up), act)()
+
+                getattr(block(i, 2, across), act)()
+
+            @pl.when(line + d < length)
+            def _():
+                i = me + 2 * d
+                if begin:
+                    block(i, 1, across).wait_recv()
+
+                @pl.when(has_down)
+                def _():
+                    getattr(block(i, 1, down), act)()
+
+                getattr(block(i, 2, across), act)()
+
+        if begin:
+            for k in range(length):
+                block(2 * k + 1 - side, 2, across).wait_recv()
+    keep.wait()
+
+
+def share_sent(sent, reps):
+    return pl.pallas_call(
+        functools.partial(share_sent_kernel, reps),
+        out_shape=jax.ShapeDtypeStruct((reps,) + sent.shape, sent.dtype),
+        in_specs=[pl.BlockSpec(memory_space=pl.ANY)],
+        out_specs=pl.BlockSpec(memory_space=pl.ANY),
+        scratch_shapes=[
+            pltpu.SemaphoreType.DMA((reps, 3)),
+            pltpu.SemaphoreType.DMA((reps,)),
+            pltpu.SemaphoreType.DMA,
+        ],
+        compiler_params=pltpu.CompilerParams(collective_id=0, has_side_effects=True),
+        name="share_sent",
+    )(sent)
+
+
+PIECES = 8
+
+
+def share_rows_kernel(shards, mine, out, send, recv, local):
+    dp, s = lax.axis_index("dp"), lax.axis_index("shard")
+    core, far = lax.rem(s, 2), s // 2
+    group = shards // 2
+    g = lax.rem(dp, 4)
+    flip1 = lambda v: v + 1 - 2 * lax.rem(v, 2)
+    flip2 = lambda v: v + 2 - 4 * lax.rem(v // 2, 2)
+    width = mine.shape[1] // PIECES
+    inner, side, deep = {"shard": flip1(s)}, {"dp": flip1(dp)}, {"dp": flip2(dp)}
+    outer = [2 * lax.rem(far + k, group) + core for k in range(1, group)]
+
+    barrier = pltpu.get_barrier_semaphore()
+    for peer in [inner, side, deep] + [{"shard": o} for o in outer]:
+        pl.semaphore_signal(barrier, inc=1, device_id=peer, device_id_type=MESH)
+    pl.semaphore_wait(barrier, 3 + len(outer))
+
+    lanes = lambda j: pl.ds(pl.multiple_of(j * width, BLK), width)
+
+    def piece(o, j, way, peer):
+        ref = out.at[o, :, lanes(j)]
+        return copy_to(ref, ref, send.at[o, j, way], recv.at[o, j], peer)
+
+    def own(j, k):
+        return copy_to(
+            mine.at[:, lanes(j)], out.at[s, :, lanes(j)], send.at[s, j, k], recv.at[s, j], {"shard": outer[k]}
+        )
+
+    sends = []
+
+    def go(c):
+        c.start()
+        sends.append(c)
+
+    for half in (0, 4):
+        for k in range(len(outer)):
+            go(own(g + half, k))
+    go(copy_to(mine, out.at[s], send.at[s, 0, group], recv.at[s, PIECES], inner))
+    keep = pltpu.make_async_copy(mine, out.at[s], local)
+    keep.start()
+
+    for half in (0, 4):
+        for o in outer:
+            j = g + half
+            piece(o, j, 0, inner).wait_recv()
+            go(piece(o, j, 0, side))
+            go(piece(o, j, 1, deep))
+            go(piece(o, j, 2, inner))
+    a, b, c = flip1(g), flip2(g), flip2(flip1(g))
+    for half in (0, 4):
+        for o in outer:
+            piece(o, a + half, 0, inner).wait_recv()
+            if half == 0:
+                go(piece(o, a + half, 1, deep))
+            go(piece(o, a + half, 2, inner))
+            piece(o, b + half, 0, inner).wait_recv()
+            if half == 4:
+                go(piece(o, b + half, 0, side))
+            go(piece(o, b + half, 2, inner))
+    for half in (0, 4):
+        for o in outer:
+            piece(o, c + half, 0, inner).wait_recv()
+            go(piece(o, c + half, 2, inner))
+    for o in outer:
+        for j in range(PIECES):
+            piece(flip1(o), j, 0, inner).wait_recv()
+    other = flip1(s)
+    copy_to(mine, out.at[other], send.at[other, 0, 0], recv.at[other, PIECES], inner).wait_recv()
+    for x in sends:
+        x.wait_send()
+    keep.wait()
+
+
+def share_rows(copy, shards):
+    rows, D = copy.shape
+    out = pl.pallas_call(
+        functools.partial(share_rows_kernel, shards),
+        out_shape=jax.ShapeDtypeStruct((shards, rows, D), copy.dtype),
+        in_specs=[pl.BlockSpec(memory_space=pl.ANY)],
+        out_specs=pl.BlockSpec(memory_space=pl.ANY),
+        scratch_shapes=[
+            pltpu.SemaphoreType.DMA((shards, PIECES, max(3, shards))),
+            pltpu.SemaphoreType.DMA((shards, PIECES + 1)),
+            pltpu.SemaphoreType.DMA,
+        ],
+        compiler_params=pltpu.CompilerParams(collective_id=1, has_side_effects=True),
+        name="share_rows",
+    )(copy)
+    return out.reshape(shards * rows, D)
+
+
 def on_device(grads, momentum, param, thresholds, sel_blocks, counts):
     rows, D = param.shape
     per_row = D // BLK
@@ -201,9 +390,9 @@
     new_momentum, sent = encode(
         momentum[0], grads[0], thresholds[:, None], sel, place, counts, fwd, inv, width
     )
-    gathered = lax.all_gather(sent, "dp", axis=0, tiled=False)
+    gathered = share_sent(sent, sel.shape[0])
     new_param, copy = apply(place, gathered, param, inv, width)
-    compute_copy = lax.all_gather(copy, "shard", axis=0, tiled=True)
+    compute_copy = share_rows(copy, lax.axis_size("shard"))
     return (new_momentum[None], new_param, compute_copy)
 
 

time: 161 us -> 133 us (0.83)
  waiting for transfers between devices: 91.9 us -> 0 us
  Pallas kernels: 42.7 us -> 120 us
  between operations: 14 us -> 0.65 us
    all_gather x2 -> x0, waiting for transfers between devices: 91.9 us -> none  [the longest x1 47 us: on_device(): gathered = lax.all_gather(sent, 'dp', axis=0, tiled=False)]
    pallas_call x0 -> x2, Pallas kernels: none -> 77.5 us  [the longest x1 51.7 us: share_rows(): pl.pallas_call(functools.partial(share_rows_kernel, shards), out_shape=ja...]
  transfers between devices with their start and end apart: 2 -> 0, of which waited for: 2 -> 0; matrix products, arithmetic and copies ran while one was open for 0% -> 0% of each run, Pallas kernels for 0% -> 0%
where the time goes in v2:
time: 133 us
  Pallas kernels  120 us (90%)
  local copies, waits for them, and re-layouts  10.2 us (8%)
  other arithmetic  1.36 us (1%)
    pallas_call x1, Pallas kernels, share_rows(): pl.pallas_call(functools.partial(share_rows_kernel, shards), out_shape=ja...  51.7 us
    pallas_call x1, Pallas kernels, apply(): pl.pallas_call(functools.partial(apply_kernel, reps), grid=(reps + D // w...  31.9 us
    pallas_call x1, Pallas kernels, share_sent(): pl.pallas_call(functools.partial(share_sent_kernel, reps), out_shape=jax....  25.8 us
    pallas_call x1, Pallas kernels, encode(): pl.pallas_call(functools.partial(encode_kernel, D // BLK), grid=(D // wid...  10.9 us
    unnamed x3, local copies, waits for them, and re-layouts  8.85 us

profile of v2, /device:TPU:0, one launch (start us, length us, event | category | flops | bytes accessed | tf_op | source)
XLA Modules:
  0.0 132.5 jit_solution(12027028601818478101)
XLA Ops:
  0.6 1.3 copy.12.counts
  1.9 1.4 %fusion.1.place = s32[8,768]{1,0:T(8,128)} fusion(s32[8,1,768]{2,1,0:T(1,128)} %param.13), kind=kLoop, calls=%fused_computation.6 | loop fusion | flops 129024 | bytes 49152 | tf_op jit(solution)/shard_map/add | solution.py:389
  3.3 1.3 %copy.17 = s32[8,1,768]{2,0,1:T(8,128)} copy(s32[8,1,768]{2,1,0:T(1,128)} %param.13) | data formatting | bytes 49152
  4.6 1.4 %copy.11.thr = f32[96,1]{1,0:T(8,128)} copy(f32[96,1]{0,1:T(1,128)} %bitcast.14) | data formatting | bytes 768 | tf_op jit(solution)/shard_map/broadcast_in_dim | solution.py:391
  6.0 10.9 %encode.1 = (f32[96,8192]{1,0:T(8,128)}, bf16[768,128]{1,0:T(8,128)(2,1)}) custom-call(f32[96,8192]{1,0:T(8,128)} %bitcast.11, bf16[96,8192]{1,0:T(8,128)(2,1)} %bitcast.12, f32[96,1]{1,0:T(8,128)} %copy.11.thr, s32[8,768]{1,0:T(8,128)} %bitcast.13, s32[8,768]{1,0:T(8,128)} %fusion.1.place, s32[8,1]{1,0:T(8,128)} %copy.12.counts, ...), custom_call_target="tpu_custom_call" | custom-call | tf_op jit(solution)/shard_map/encode/pallas_call | solution.py:101
  16.9 25.8 %share_sent.1.sent = bf16[8,768,128]{2,1,0:T(8,128)(2,1)} custom-call(bf16[768,128]{1,0:T(8,128)(2,1)} %get-tuple-element.8.mine), custom_call_target="tpu_custom_call" | custom-call | tf_op jit(solution)/shard_map/share_sent/pallas_call | solution.py:275
  42.7 31.9 %apply.1 = (f32[96,8192]{1,0:T(8,128)}, bf16[96,8192]{1,0:T(8,128)(2,1)}) custom-call(s32[8,768]{1,0:T(8,128)} %fusion.1.place, bf16[8,768,128]{2,1,0:T(8,128)(2,1)} %share_sent.1.sent, f32[96,8192]{1,0:T(8,128)} %param.15, bf16[256,256]{1,0:T(8,128)(2,1)} %constant.35.clone.inv), custom_call_target="tpu_custom_call" | custom-call | tf_op jit(solution)/shard_map/apply/pallas_call | solution.py:171
  74.6 51.7 %share_rows.1 = bf16[4,96,8192]{2,1,0:T(8,128)(2,1)} custom-call(bf16[96,8192]{1,0:T(8,128)(2,1)} %get-tuple-element.10.mine), custom_call_target="tpu_custom_call" | custom-call | tf_op jit(solution)/shard_map/share_rows/pallas_call | solution.py:367
  126.3 6.2 %copy.19 = bf16[384,8192]{1,0:T(8,128)(2,1)} copy(bf16[384,8192]{1,0:T(8,128)(2,1)} %bitcast.10) | data formatting | bytes 12582912

commit v3 on v2

--- a/solution.py
+++ b/solution.py
@@ -46,20 +46,23 @@
     return jnp.concatenate([x[:, c * BLK : (c + 1) * BLK] for c in range(x.shape[1] // BLK)], axis=0)
 
 
-def encode_kernel(per_row, mom, grad, thr, sel, place, counts, fwd, inv, newmom, sent, rowhot, dense, picked):
+def encode_kernel(per_row, mom, grad, thr, sel, place, counts, fwd, inv, newmom, sent, rowhot, dense, picked, level):
     step = pl.program_id(0)
     replica = lax.axis_index("dp")
     rows, width = mom.shape
-    slots = sel.shape[1]
+    slots = sel.shape[2]
     cols = width // BLK
-    ids = sel[pl.ds(replica, 1), :]
+    ids = sel[replica]
 
     @pl.when(step == 0)
     def _():
-        live = lax.broadcasted_iota(jnp.int32, (1, slots), 1) < counts[replica, 0]
+        live = lax.broadcasted_iota(jnp.int32, (1, slots), 1) < counts[replica]
         row_of = jnp.where(live, ids // per_row, -1)
         hot = row_of == lax.broadcasted_iota(jnp.int32, (rows, slots), 0)
         rowhot[...] = jnp.where(hot, 1.0, 0.0).astype(jnp.bfloat16)
+        eye = lax.broadcasted_iota(jnp.int32, (rows, rows), 0) == lax.broadcasted_iota(jnp.int32, (rows, rows), 1)
+        column = jnp.sum(jnp.where(eye, thr[...], 0.0), axis=1, keepdims=True)
+        level[...] = jnp.broadcast_to(column, level.shape)
 
     colhot = ids % per_row == step * cols + lax.broadcasted_iota(jnp.int32, (max(cols, 8), slots), 0)
     mask = lax.dot_general(
@@ -70,11 +73,12 @@
     )
     blended = tiles(beta_decay * mom[...] + grad[...].astype(jnp.float32))
     coef = both(split(blended), fwd[...])
-    t = jnp.concatenate([jnp.broadcast_to(thr[...], (rows, BLK))] * cols, axis=0)
+    t = jnp.concatenate([level[...]] * cols, axis=0)
     shrunk = coef - jnp.clip(coef, -t, t)
     keep = jnp.concatenate([jnp.broadcast_to(mask[:, c : c + 1], (rows, BLK)) for c in range(cols)], axis=0)
     kept = jnp.where(keep > 0.5, shrunk, 0.0)
-    dense[pl.ds(pl.multiple_of(step * (cols * rows), 8), cols * rows), :] = kept
+    for c in range(cols):
+        dense[pl.ds(step * cols + c, rows, stride=per_row), :] = kept[c * rows : (c + 1) * rows]
     out = blended - both(kept.astype(jnp.bfloat16), inv[:BLK, :])
     for c in range(cols):
         newmom[:, c * BLK : (c + 1) * BLK] = out[c * rows : (c + 1) * rows]
@@ -83,7 +87,7 @@
     def _():
         def pick(i, carry):
             base = i * UNROLL
-            got = [dense[pl.ds(place[replica, base + u], 1), :] for u in range(UNROLL)]
+            got = [dense[pl.ds(place[replica, 0, base + u], 1), :] for u in range(UNROLL)]
             for u in range(UNROLL):
                 picked[pl.ds(base + u, 1), :] = got[u]
             return carry
@@ -92,9 +96,9 @@
         sent[...] = picked[...].astype(jnp.bfloat16)
 
 
-def encode(mom, grad, thr, sel, place, counts, fwd, inv, width):
+def encode(mom, grad, thr, sel, counts, fwd, inv, width):
     rows, D = mom.shape
-    reps, slots = sel.shape
+    slots = sel.shape[2]
     col = pl.BlockSpec((rows, width), lambda i: (0, i))
     whole = lambda a: pl.BlockSpec(a.shape, lambda i: (0,) * a.ndim)
     smem = pl.BlockSpec(memory_space=pltpu.SMEM)
@@ -111,9 +115,10 @@
             pltpu.VMEM((rows, slots), jnp.bfloat16),
             pltpu.VMEM((rows * (D // BLK), BLK), jnp.float32),
             pltpu.VMEM((slots, BLK), jnp.float32),
+            pltpu.VMEM((rows, BLK), jnp.float32),
         ],
         name="encode",
-    )(mom, grad, thr, sel, place, counts, fwd, inv)
+    )(mom, grad, thr, sel, sel, counts, fwd, inv)
 
 
 def apply_kernel(reps, place, sent, param, inv, newparam, copy, total, wide, scale):
@@ -133,7 +138,7 @@
 
         def put(i, carry):
             base = pl.multiple_of(i * UNROLL, UNROLL)
-            at = [place[step, base + u] for u in range(UNROLL)]
+            at = [place[step, 0, base + u] for u in range(UNROLL)]
             new = [total[pl.ds(at[u], 1), :] + wide[pl.ds(base + u, 1), :] for u in range(UNROLL)]
             for u in range(UNROLL):
                 total[pl.ds(at[u], 1), :] = new[u]
@@ -144,7 +149,7 @@
     @pl.when(step == reps)
     def _():
         def square(c, acc):
-            a = total[pl.ds(pl.multiple_of(c * rows, 8), rows), :] * (1.0 / reps)
+            a = total[pl.ds(c, rows, stride=all_cols), :] * (1.0 / reps)
             return acc + a * a
 
         acc = lax.fori_loop(0, all_cols, square, jnp.zeros((rows, BLK), jnp.float32), unroll=4)
@@ -153,8 +158,10 @@
 
     @pl.when(step >= reps)
     def _():
-        at = pl.multiple_of((step - reps) * (cols * rows), 8)
-        averaged = total[pl.ds(at, cols * rows), :] * (1.0 / reps)
+        first = (step - reps) * cols
+        averaged = jnp.concatenate(
+            [total[pl.ds(first + c, rows, stride=all_cols), :] for c in range(cols)], axis=0
+        ) * (1.0 / reps)
         direction = both(split(averaged), inv[...])
         for c in range(cols):
             lanes = slice(c * BLK, (c + 1) * BLK)
@@ -275,7 +282,7 @@
     return pl.pallas_call(
         functools.partial(share_sent_kernel, reps),
         out_shape=jax.ShapeDtypeStruct((reps,) + sent.shape, sent.dtype),
-        in_specs=[pl.BlockSpec(memory_space=pl.ANY)],
+        in_specs=[pl.BlockSpec(memory_space=pltpu.VMEM)],
         out_specs=pl.BlockSpec(memory_space=pl.ANY),
         scratch_shapes=[
             pltpu.SemaphoreType.DMA((reps, 3)),
@@ -367,7 +374,7 @@
     out = pl.pallas_call(
         functools.partial(share_rows_kernel, shards),
         out_shape=jax.ShapeDtypeStruct((shards, rows, D), copy.dtype),
-        in_specs=[pl.BlockSpec(memory_space=pl.ANY)],
+        in_specs=[pl.BlockSpec(memory_space=pltpu.VMEM)],
         out_specs=pl.BlockSpec(memory_space=pl.ANY),
         scratch_shapes=[
             pltpu.SemaphoreType.DMA((shards, PIECES, max(3, shards))),
@@ -382,16 +389,13 @@
 
 def on_device(grads, momentum, param, thresholds, sel_blocks, counts):
     rows, D = param.shape
-    per_row = D // BLK
     width = min(1024, D)
     fwd, inv = (jnp.asarray(t) for t in tables())
-    sel = sel_blocks[:, 0, :]
-    place = (sel % per_row) * rows + sel // per_row
     new_momentum, sent = encode(
-        momentum[0], grads[0], thresholds[:, None], sel, place, counts, fwd, inv, width
+        momentum[0], grads[0], thresholds[None, :], sel_blocks, counts[:, 0], fwd, inv, width
     )
-    gathered = share_sent(sent, sel.shape[0])
-    new_param, copy = apply(place, gathered, param, inv, width)
+    gathered = share_sent(sent, sel_blocks.shape[0])
+    new_param, copy = apply(sel_blocks, gathered, param, inv, width)
     compute_copy = share_rows(copy, lax.axis_size("shard"))
     return (new_momentum[None], new_param, compute_copy)
 

time: 133 us -> 104 us (0.78)
  Pallas kernels: 120 us -> 96.2 us
  local copies, waits for them, and re-layouts: 10.2 us -> 6.2 us
  other arithmetic: 1.36 us -> 0 us
    pallas_call x1, Pallas kernels: 51.7 us -> 27.3 us  [share_rows(): pl.pallas_call(functools.partial(share_rows_kernel, shards), out_shape=ja...]
    unnamed x3 -> x1, local copies, waits for them, and re-layouts: 8.85 us -> 6.2 us
    pallas_call x1, Pallas kernels: 31.9 us -> 30.4 us  [apply(): pl.pallas_call(functools.partial(apply_kernel, reps), grid=(reps + D // w...]
    broadcast_in_dim x1 -> x0, local copies, waits for them, and re-layouts: 1.37 us -> none  [on_device(): thresholds[:, None]]
    add x1 -> x0, other arithmetic: 1.36 us -> none  [on_device(): place = sel % per_row * rows + sel // per_row]
where the time goes in v3:
time: 104 us; the launch traced here: 103 us
  Pallas kernels  96.2 us (92%)
  local copies, waits for them, and re-layouts  6.2 us (6%)
    pallas_call x1, Pallas kernels, apply(): pl.pallas_call(functools.partial(apply_kernel, reps), grid=(reps + D // w...  30.4 us
    pallas_call x1, Pallas kernels, share_rows(): pl.pallas_call(functools.partial(share_rows_kernel, shards), out_shape=ja...  27.3 us
    pallas_call x1, Pallas kernels, share_sent(): pl.pallas_call(functools.partial(share_sent_kernel, reps), out_shape=jax....  26.5 us
    pallas_call x1, Pallas kernels, encode(): pl.pallas_call(functools.partial(encode_kernel, D // BLK), grid=(D // wid...  12 us
    unnamed x1, local copies, waits for them, and re-layouts  6.2 us

profile of v3, /device:TPU:0, one launch (start us, length us, event | category | flops | bytes accessed | tf_op | source)
XLA Modules:
  0.0 103.0 jit_solution(4893988942705416434)
XLA Ops:
  0.6 12.0 %encode.1 = (f32[96,8192]{1,0:T(8,128)}, bf16[768,128]{1,0:T(8,128)(2,1)}) custom-call(f32[96,8192]{1,0:T(8,128)} %bitcast.7, bf16[96,8192]{1,0:T(8,128)(2,1)} %bitcast.8, f32[1,96]{1,0:T(1,128)} %bitcast.9, s32[8,1,768]{2,1,0:T(1,128)} %place.3, s32[8,1,768]{2,1,0:T(1,128)} %place.3, s32[8]{0:T(128)} %bitcast.10, bf16[256,256]{1,0:T(8,128)(2,1)} %constant.4.clone.fwd, ...), custom_call_target="tpu_custom_call" | custom-call | tf_op jit(solution)/shard_map/encode/pallas_call | solution.py:105
  12.6 26.5 %share_sent.1.sent = bf16[8,768,128]{2,1,0:T(8,128)(2,1)} custom-call(bf16[768,128]{1,0:T(8,128)(2,1)} %get-tuple-element.8.mine), custom_call_target="tpu_custom_call" | custom-call | tf_op jit(solution)/shard_map/share_sent/pallas_call | solution.py:282
  39.1 30.4 %apply.1 = (f32[96,8192]{1,0:T(8,128)}, bf16[96,8192]{1,0:T(8,128)(2,1)}) custom-call(s32[8,1,768]{2,1,0:T(1,128)} %place.3, bf16[8,768,128]{2,1,0:T(8,128)(2,1)} %share_sent.1.sent, f32[96,8192]{1,0:T(8,128)} %param.15, bf16[256,256]{1,0:T(8,128)(2,1)} %constant.5.clone.inv), custom_call_target="tpu_custom_call" | custom-call | tf_op jit(solution)/shard_map/apply/pallas_call | solution.py:178
  69.5 27.3 %share_rows.1 = bf16[4,96,8192]{2,1,0:T(8,128)(2,1)} custom-call(bf16[96,8192]{1,0:T(8,128)(2,1)} %get-tuple-element.10.mine), custom_call_target="tpu_custom_call" | custom-call | tf_op jit(solution)/shard_map/share_rows/pallas_call | solution.py:374
  96.8 6.2 %copy.12 = bf16[384,8192]{1,0:T(8,128)(2,1)} copy(bf16[384,8192]{1,0:T(8,128)(2,1)} %bitcast.6) | data formatting | bytes 12582912

commit v4 on v3

--- a/solution.py
+++ b/solution.py
@@ -121,81 +121,33 @@
     )(mom, grad, thr, sel, sel, counts, fwd, inv)
 
 
-def apply_kernel(reps, place, sent, param, inv, newparam, copy, total, wide, scale):
-    step = pl.program_id(0)
+def apply_kernel(total, scale, param, inv, newparam, copy):
     rows, width = param.shape
-    slots = wide.shape[0]
     cols = width // BLK
-    all_cols = total.shape[0] // rows
-
-    @pl.when(step == 0)
-    def _():
-        total[...] = jnp.zeros_like(total)
-
-    @pl.when(step < reps)
-    def _():
-        wide[...] = sent[0].astype(jnp.float32)
-
-        def put(i, carry):
-            base = pl.multiple_of(i * UNROLL, UNROLL)
-            at = [place[step, 0, base + u] for u in range(UNROLL)]
-            new = [total[pl.ds(at[u], 1), :] + wide[pl.ds(base + u, 1), :] for u in range(UNROLL)]
-            for u in range(UNROLL):
-                total[pl.ds(at[u], 1), :] = new[u]
-            return carry
-
-        lax.fori_loop(0, slots // UNROLL, put, 0)
-
-    @pl.when(step == reps)
-    def _():
-        def square(c, acc):
-            a = total[pl.ds(c, rows, stride=all_cols), :] * (1.0 / reps)
-            return acc + a * a
-
-        acc = lax.fori_loop(0, all_cols, square, jnp.zeros((rows, BLK), jnp.float32), unroll=4)
-        mean = jnp.sum(acc, axis=1, keepdims=True) * (1.0 / (all_cols * BLK))
-        scale[...] = jnp.broadcast_to(lax.rsqrt(mean + 1e-06), scale.shape)
-
-    @pl.when(step >= reps)
-    def _():
-        first = (step - reps) * cols
-        averaged = jnp.concatenate(
-            [total[pl.ds(first + c, rows, stride=all_cols), :] for c in range(cols)], axis=0
-        ) * (1.0 / reps)
-        direction = both(split(averaged), inv[...])
-        for c in range(cols):
-            lanes = slice(c * BLK, (c + 1) * BLK)
-            update = jnp.tanh(direction[c * rows : (c + 1) * rows] * scale[...])
-            new = param[:, lanes] - step_size * update
-            newparam[:, lanes] = new
-            copy[:, lanes] = new.astype(jnp.bfloat16)
-
-
-def apply(place, sent, param, inv, width):
+    direction = both(split(tiles(total[...])), inv[...])
+    for c in range(cols):
+        lanes = slice(c * BLK, (c + 1) * BLK)
+        update = jnp.tanh(direction[c * rows : (c + 1) * rows] * scale[...])
+        new = param[:, lanes] - step_size * update
+        newparam[:, lanes] = new
+        copy[:, lanes] = new.astype(jnp.bfloat16)
+
+
+def apply(total, scale, param, inv, width):
     rows, D = param.shape
-    reps, slots, _ = sent.shape
-    col = pl.BlockSpec((rows, width), lambda i: (0, jnp.maximum(i - reps, 0)))
+    col = pl.BlockSpec((rows, width), lambda i: (0, i))
+    whole = lambda a: pl.BlockSpec(a.shape, lambda i: (0,) * a.ndim)
     return pl.pallas_call(
-        functools.partial(apply_kernel, reps),
-        grid=(reps + D // width,),
-        in_specs=[
-            pl.BlockSpec(memory_space=pltpu.SMEM),
-            pl.BlockSpec((1, slots, BLK), lambda i: (jnp.minimum(i, reps - 1), 0, 0)),
-            col,
-            pl.BlockSpec(inv.shape, lambda i: (0, 0)),
-        ],
+        apply_kernel,
+        grid=(D // width,),
+        in_specs=[col, whole(scale), col, whole(inv)],
         out_specs=[col, col],
         out_shape=[
             jax.ShapeDtypeStruct(param.shape, jnp.float32),
             jax.ShapeDtypeStruct(param.shape, jnp.bfloat16),
         ],
-        scratch_shapes=[
-            pltpu.VMEM((rows * (D // BLK), BLK), jnp.float32),
-            pltpu.VMEM((slots, BLK), jnp.float32),
-            pltpu.VMEM((rows, BLK), jnp.float32),
-        ],
         name="apply",
-    )(place, sent, param, inv)
+    )(total, scale, param, inv)
 
 
 MESH = pl.DeviceIdType.MESH
@@ -207,10 +159,13 @@
     )
 
 
-def share_sent_kernel(reps, mine, out, send, recv, local):
+def sum_sent_kernel(reps, mine, sel, total, scale, buf, send, recv):
     me = lax.axis_index("dp")
     line, side = me // 2, lax.rem(me, 2)
     length = reps // 2
+    rows, D = total.shape
+    per_row = D // BLK
+    slots = mine.shape[0]
     up, down, across = {"dp": me + 2}, {"dp": me - 2}, {"dp": me + 1 - 2 * side}
     has_up, has_down = line < length - 1, line > 0
 
@@ -228,15 +183,10 @@
     pl.semaphore_wait(barrier, 1 + jnp.where(has_up, 1, 0) + jnp.where(has_down, 1, 0))
 
     def block(i, way, peer, own=False):
-        src = mine if own else out.at[i]
-        return copy_to(src, out.at[i], send.at[i, way], recv.at[i], peer)
-
-    for act in ("start", "wait_send"):
-        begin = act == "start"
-        if begin:
-            keep = pltpu.make_async_copy(mine, out.at[me], local)
-            keep.start()
-
+        src = mine if own else buf.at[i]
+        return copy_to(src, buf.at[i], send.at[i, way], recv.at[i], peer)
+
+    def first(act):
         @pl.when(has_up)
         def _():
             getattr(block(me, 0, up, True), act)()
@@ -246,52 +196,127 @@
             getattr(block(me, 1, down, True), act)()
 
         getattr(block(me, 2, across, True), act)()
-        for d in range(1, length):
-
-            @pl.when(line >= d)
+
+    def relay(d, act):
+        @pl.when(line >= d)
+        def _():
+            i = me - 2 * d
+            if act == "start":
+                block(i, 0, across).wait_recv()
+
+            @pl.when(has_up)
             def _():
-                i = me - 2 * d
-                if begin:
-                    block(i, 0, across).wait_recv()
-
-                @pl.when(has_up)
+                getattr(block(i, 0, up), act)()
+
+            getattr(block(i, 2, across), act)()
+
+        @pl.when(line + d < length)
+        def _():
+            i = me + 2 * d
+            if act == "start":
+                block(i, 1, across).wait_recv()
+
+            @pl.when(has_down)
+            def _():
+                getattr(block(i, 1, down), act)()
+
+            getattr(block(i, 2, across), act)()
+
+    first("start")
+    total[...] = jnp.zeros_like(total)
+    group = min(8, per_row // 2)
+
+    def accumulate(i):
+        ids = sel[i]
+        col = ids % per_row
+        hot = ids // per_row == lax.broadcasted_iota(jnp.int32, (rows, slots), 0)
+        rowhot = jnp.where(hot, 1.0, 0.0).astype(jnp.bfloat16)
+        odd = jnp.transpose(jnp.broadcast_to((col % 2).astype(jnp.float32), (BLK, slots)))
+        right = odd.astype(jnp.bfloat16)
+        values = buf[i]
+        rhs = jnp.concatenate([values * (1.0 - odd).astype(jnp.bfloat16), values * right], axis=1)
+        pair = jnp.broadcast_to(col // 2, (16, slots))
+
+        def chunk(q, carry):
+            parts = []
+            for u in range(group):
+                pick = jnp.where(pair == q * group + u, 1.0, 0.0).astype(jnp.bfloat16)
+                parts.append(rowhot * jnp.concatenate([pick] * (rows // 16), axis=0))
+            out = jnp.dot(jnp.concatenate(parts, axis=0), rhs, preferred_element_type=jnp.float32)
+            for u in range(group):
+                at = pl.ds(pl.multiple_of((q * group + u) * (2 * BLK), BLK), 2 * BLK)
+                total[:, at] += out[u * rows : (u + 1) * rows]
+            return carry
+
+        lax.fori_loop(0, per_row // 2 // group, chunk, 0)
+
+    buf[me] = mine[...]
+
+    def step(d, carry):
+        @pl.when(d > 0)
+        def _():
+            relay(d, "start")
+
+        def visit(t, carry):
+            other = t // 2
+            far = d - other
+            at = line + (2 * lax.rem(t, 2) - 1) * far
+            twin = (far == 0) & (lax.rem(t, 2) == 1)
+
+            @pl.when((far >= 0) & (at >= 0) & (at < length) & jnp.logical_not(twin))
+            def _():
+                i = 2 * at + side + other * (1 - 2 * side)
+
+                @pl.when(other == 1)
                 def _():
-                    getattr(block(i, 0, up), act)()
-
-                getattr(block(i, 2, across), act)()
-
-            @pl.when(line + d < length)
-            def _():
-                i = me + 2 * d
-                if begin:
-                    block(i, 1, across).wait_recv()
-
-                @pl.when(has_down)
-                def _():
-                    getattr(block(i, 1, down), act)()
-
-                getattr(block(i, 2, across), act)()
-
-        if begin:
-            for k in range(length):
-                block(2 * k + 1 - side, 2, across).wait_recv()
-    keep.wait()
-
-
-def share_sent(sent, reps):
+                    block(i, 2, across).wait_recv()
+
+                accumulate(i)
+
+            return carry
+
+        lax.fori_loop(0, 4, visit, 0)
+        return carry
+
+    lax.fori_loop(0, length + 1, step, 0)
+    first("wait_send")
+
+    def drain(d, carry):
+        relay(d, "wait_send")
+        return carry
+
+    lax.fori_loop(1, length, drain, 0)
+
+    def square(c, acc):
+        lanes = pl.ds(pl.multiple_of(c * BLK, BLK), BLK)
+        a = total[:, lanes] * (1.0 / reps)
+        total[:, lanes] = a
+        return acc + a * a
+
+    acc = lax.fori_loop(0, per_row, square, jnp.zeros((rows, BLK), jnp.float32), unroll=4)
+    mean = jnp.sum(acc, axis=1, keepdims=True) * (1.0 / D)
+    scale[...] = jnp.broadcast_to(lax.rsqrt(mean + 1e-06), scale.shape)
+
+
+def sum_sent(sent, sel, rows, D):
+    reps = sel.shape[0]
+    vmem = pl.BlockSpec(memory_space=pltpu.VMEM)
     return pl.pallas_call(
-        functools.partial(share_sent_kernel, reps),
-        out_shape=jax.ShapeDtypeStruct((reps,) + sent.shape, sent.dtype),
-        in_specs=[pl.BlockSpec(memory_space=pltpu.VMEM)],
-        out_specs=pl.BlockSpec(memory_space=pl.ANY),
+        functools.partial(sum_sent_kernel, reps),
+        out_shape=[
+            jax.ShapeDtypeStruct((rows, D), jnp.float32),
+            jax.ShapeDtypeStruct((rows, BLK), jnp.float32),
+        ],
+        in_specs=[vmem, vmem],
+        out_specs=[vmem, vmem],
         scratch_shapes=[
+            pltpu.VMEM((reps,) + sent.shape, sent.dtype),
             pltpu.SemaphoreType.DMA((reps, 3)),
             pltpu.SemaphoreType.DMA((reps,)),
-            pltpu.SemaphoreType.DMA,
         ],
         compiler_params=pltpu.CompilerParams(collective_id=0, has_side_effects=True),
-        name="share_sent",
-    )(sent)
+        name="sum_sent",
+    )(sent, sel)
 
 
 PIECES = 8
@@ -394,8 +419,8 @@
     new_momentum, sent = encode(
         momentum[0], grads[0], thresholds[None, :], sel_blocks, counts[:, 0], fwd, inv, width
     )
-    gathered = share_sent(sent, sel_blocks.shape[0])
-    new_param, copy = apply(sel_blocks, gathered, param, inv, width)
+    total, scale = sum_sent(sent, sel_blocks, rows, D)
+    new_param, copy = apply(total, scale, param, inv, width)
     compute_copy = share_rows(copy, lax.axis_size("shard"))
     return (new_momentum[None], new_param, compute_copy)
 

time: 104 us -> 87.2 us (0.84)
  Pallas kernels: 96.2 us -> 79.8 us
    pallas_call x2, Pallas kernels: 56.9 us -> 40.5 us  [the longest x1 32.3 us: sum_sent(): pl.pallas_call(functools.partial(sum_sent_kernel, reps), out_shape=[jax.S...]
where the time goes in v4:
time: 87.2 us; the launch traced here: 86.6 us
  Pallas kernels  79.8 us (92%)
  local copies, waits for them, and re-layouts  6.2 us (7%)
    pallas_call x1, Pallas kernels, sum_sent(): pl.pallas_call(functools.partial(sum_sent_kernel, reps), out_shape=[jax.S...  32.3 us
    pallas_call x1, Pallas kernels, share_rows(): pl.pallas_call(functools.partial(share_rows_kernel, shards), out_shape=ja...  27.3 us
    pallas_call x1, Pallas kernels, encode(): pl.pallas_call(functools.partial(encode_kernel, D // BLK), grid=(D // wid...  12 us
    pallas_call x1, Pallas kernels, apply(): pl.pallas_call(apply_kernel, grid=(D // width,), in_specs=[col, whole(sca...  8.14 us
    unnamed x1, local copies, waits for them, and re-layouts  6.2 us

profile of v4, /device:TPU:0, one launch (start us, length us, event | category | flops | bytes accessed | tf_op | source)
XLA Modules:
  0.0 86.6 jit_solution(330745562006930256)
XLA Ops:
  0.6 12.0 %encode.1 = (f32[96,8192]{1,0:T(8,128)}, bf16[768,128]{1,0:T(8,128)(2,1)}) custom-call(f32[96,8192]{1,0:T(8,128)} %bitcast.7, bf16[96,8192]{1,0:T(8,128)(2,1)} %bitcast.8, f32[1,96]{1,0:T(1,128)} %bitcast.9, s32[8,1,768]{2,1,0:T(1,128)} %sel.3, s32[8,1,768]{2,1,0:T(1,128)} %sel.3, s32[8]{0:T(128)} %bitcast.10, bf16[256,256]{1,0:T(8,128)(2,1)} %constant.4.clone.fwd, ...), custom_call_target="tpu_custom_call" | custom-call | tf_op jit(solution)/shard_map/encode/pallas_call | solution.py:105
  12.6 32.3 %sum_sent.1 = (f32[96,8192]{1,0:T(8,128)}, f32[96,128]{1,0:T(8,128)}) custom-call(bf16[768,128]{1,0:T(8,128)(2,1)} %get-tuple-element.10.mine, s32[8,1,768]{2,1,0:T(1,128)} %sel.3), custom_call_target="tpu_custom_call" | custom-call | tf_op jit(solution)/shard_map/sum_sent/pallas_call | solution.py:304
  45.0 8.1 %apply.1 = (f32[96,8192]{1,0:T(8,128)}, bf16[96,8192]{1,0:T(8,128)(2,1)}) custom-call(f32[96,8192]{1,0:T(8,128)} %get-tuple-element.11.total, f32[96,128]{1,0:T(8,128)} %get-tuple-element.12.scale, f32[96,8192]{1,0:T(8,128)} %param.15, bf16[256,256]{1,0:T(8,128)(2,1)} %constant.5.clone.inv), custom_call_target="tpu_custom_call" | custom-call | tf_op jit(solution)/shard_map/apply/pallas_call | solution.py:140
  53.1 27.3 %share_rows.1 = bf16[4,96,8192]{2,1,0:T(8,128)(2,1)} custom-call(bf16[96,8192]{1,0:T(8,128)(2,1)} %get-tuple-element.14.mine), custom_call_target="tpu_custom_call" | custom-call | tf_op jit(solution)/shard_map/share_rows/pallas_call | solution.py:399
  80.5 6.2 %copy.12 = bf16[384,8192]{1,0:T(8,128)(2,1)} copy(bf16[384,8192]{1,0:T(8,128)(2,1)} %bitcast.6) | data formatting | bytes 12582912

commit v5 on v4

--- a/solution.py
+++ b/solution.py
@@ -121,35 +121,6 @@
     )(mom, grad, thr, sel, sel, counts, fwd, inv)
 
 
-def apply_kernel(total, scale, param, inv, newparam, copy):
-    rows, width = param.shape
-    cols = width // BLK
-    direction = both(split(tiles(total[...])), inv[...])
-    for c in range(cols):
-        lanes = slice(c * BLK, (c + 1) * BLK)
-        update = jnp.tanh(direction[c * rows : (c + 1) * rows] * scale[...])
-        new = param[:, lanes] - step_size * update
-        newparam[:, lanes] = new
-        copy[:, lanes] = new.astype(jnp.bfloat16)
-
-
-def apply(total, scale, param, inv, width):
-    rows, D = param.shape
-    col = pl.BlockSpec((rows, width), lambda i: (0, i))
-    whole = lambda a: pl.BlockSpec(a.shape, lambda i: (0,) * a.ndim)
-    return pl.pallas_call(
-        apply_kernel,
-        grid=(D // width,),
-        in_specs=[col, whole(scale), col, whole(inv)],
-        out_specs=[col, col],
-        out_shape=[
-            jax.ShapeDtypeStruct(param.shape, jnp.float32),
-            jax.ShapeDtypeStruct(param.shape, jnp.bfloat16),
-        ],
-        name="apply",
-    )(total, scale, param, inv)
-
-
 MESH = pl.DeviceIdType.MESH
 
 
@@ -159,7 +130,23 @@
     )
 
 
-def sum_sent_kernel(reps, mine, sel, total, scale, buf, send, recv):
+CLASSES = 4
+PIECES = 16
+
+
+def exchange_kernel(
+    reps, shards, mine, sel, param, inv, newparam, rowsout, total, scale, pbuf, cbuf, buf, send, recv, send2, recv2, local
+):
+    fetch = pltpu.make_async_copy(param, pbuf, local.at[0])
+    fetch.start()
+    s = lax.axis_index("shard")
+    group = shards // 2
+    core, far = lax.rem(s, 2), s // 2
+    flip1 = lambda v: v + 1 - 2 * lax.rem(v, 2)
+    flip2 = lambda v: v + 2 - 4 * lax.rem(v // 2, 2)
+    inner = {"shard": flip1(s)}
+    outer = [2 * lax.rem(far + k, group) + core for k in range(1, group)]
+
     me = lax.axis_index("dp")
     line, side = me // 2, lax.rem(me, 2)
     length = reps // 2
@@ -180,7 +167,9 @@
     def _():
         pl.semaphore_signal(barrier, inc=1, device_id=down, device_id_type=MESH)
 
-    pl.semaphore_wait(barrier, 1 + jnp.where(has_up, 1, 0) + jnp.where(has_down, 1, 0))
+    for peer in [inner] + [{"shard": o} for o in outer]:
+        pl.semaphore_signal(barrier, inc=1, device_id=peer, device_id_type=MESH)
+    pl.semaphore_wait(barrier, 2 + len(outer) + jnp.where(has_up, 1, 0) + jnp.where(has_down, 1, 0))
 
     def block(i, way, peer, own=False):
         src = mine if own else buf.at[i]
@@ -224,7 +213,7 @@
 
     first("start")
     total[...] = jnp.zeros_like(total)
-    group = min(8, per_row // 2)
+    batch = min(8, per_row // 2)
 
     def accumulate(i):
         ids = sel[i]
@@ -239,16 +228,16 @@
 
         def chunk(q, carry):
             parts = []
-            for u in range(group):
-                pick = jnp.where(pair == q * group + u, 1.0, 0.0).astype(jnp.bfloat16)
+            for u in range(batch):
+                pick = jnp.where(pair == q * batch + u, 1.0, 0.0).astype(jnp.bfloat16)
                 parts.append(rowhot * jnp.concatenate([pick] * (rows // 16), axis=0))
             out = jnp.dot(jnp.concatenate(parts, axis=0), rhs, preferred_element_type=jnp.float32)
-            for u in range(group):
-                at = pl.ds(pl.multiple_of((q * group + u) * (2 * BLK), BLK), 2 * BLK)
+            for u in range(batch):
+                at = pl.ds(pl.multiple_of((q * batch + u) * (2 * BLK), BLK), 2 * BLK)
                 total[:, at] += out[u * rows : (u + 1) * rows]
             return carry
 
-        lax.fori_loop(0, per_row // 2 // group, chunk, 0)
+        lax.fori_loop(0, per_row // 2 // batch, chunk, 0)
 
     buf[me] = mine[...]
 
@@ -279,14 +268,6 @@
         return carry
 
     lax.fori_loop(0, length + 1, step, 0)
-    first("wait_send")
-
-    def drain(d, carry):
-        relay(d, "wait_send")
-        return carry
-
-    lax.fori_loop(1, length, drain, 0)
-
     def square(c, acc):
         lanes = pl.ds(pl.multiple_of(c * BLK, BLK), BLK)
         a = total[:, lanes] * (1.0 / reps)
@@ -296,120 +277,140 @@
     acc = lax.fori_loop(0, per_row, square, jnp.zeros((rows, BLK), jnp.float32), unroll=4)
     mean = jnp.sum(acc, axis=1, keepdims=True) * (1.0 / D)
     scale[...] = jnp.broadcast_to(lax.rsqrt(mean + 1e-06), scale.shape)
-
-
-def sum_sent(sent, sel, rows, D):
+    fetch.wait()
+
+    g = lax.rem(me, CLASSES)
+    width = D // PIECES
+    deep, side_peer = {"dp": flip2(me)}, across
+    turns = PIECES // CLASSES
+
+    def lanes(j):
+        return pl.ds(pl.multiple_of(j * width, BLK), width)
+
+    def piece(o, j, way, peer):
+        ref = rowsout.at[o, :, lanes(j)]
+        return copy_to(ref, ref, send2.at[o, j, way], recv2.at[o, j], peer)
+
+    def own(j, k):
+        return copy_to(
+            cbuf.at[:, lanes(j)], rowsout.at[s, :, lanes(j)], send2.at[s, j, k], recv2.at[s, j], {"shard": outer[k]}
+        )
+
+    def compute(j):
+        direction = both(split(tiles(total[:, lanes(j)])), inv[...])
+        for c in range(width // BLK):
+            at = pl.ds(pl.multiple_of(j * width + c * BLK, BLK), BLK)
+            update = jnp.tanh(direction[c * rows : (c + 1) * rows] * scale[...])
+            new = pbuf[:, at] - step_size * update
+            pbuf[:, at] = new
+            cbuf[:, at] = new.astype(jnp.bfloat16)
+
+    def lead(k, carry):
+        compute(g + CLASSES * k)
+
+        @pl.when(k > 0)
+        def _():
+            for n in range(len(outer)):
+                own(g + CLASSES * (k - 1), n).start()
+
+        return carry
+
+    def rest(turn):
+        def one(k, carry):
+            compute(lax.rem(g + turn, CLASSES) + CLASSES * k)
+            return carry
+
+        lax.fori_loop(0, turns, one, 0)
+
+    sends = []
+
+    def go(c):
+        c.start()
+        sends.append(c)
+
+    lax.fori_loop(0, turns, lead, 0)
+    rest(1)
+    for n in range(len(outer)):
+        own(g + CLASSES * (turns - 1), n).start()
+        sends.extend(own(g + CLASSES * k, n) for k in range(turns))
+    for k in range(turns):
+        j = g + CLASSES * k
+        for o in outer:
+            piece(o, j, 0, inner).wait_recv()
+            go(piece(o, j, 0, side_peer))
+            go(piece(o, j, 1, deep))
+            go(piece(o, j, 2, inner))
+        if k < 2:
+            rest(k + 2)
+        if k == 1:
+            store = pltpu.make_async_copy(pbuf, newparam, local.at[0])
+            store.start()
+    go(copy_to(cbuf, rowsout.at[s], send2.at[s, 0, group], recv2.at[s, PIECES], inner))
+    keep = pltpu.make_async_copy(cbuf, rowsout.at[s], local.at[1])
+    keep.start()
+    a, b, c = flip1(g), flip2(g), flip2(flip1(g))
+    for k in range(turns):
+        for o in outer:
+            j = a + CLASSES * k
+            piece(o, j, 0, inner).wait_recv()
+            if k % 2 == 0:
+                go(piece(o, j, 1, deep))
+            go(piece(o, j, 2, inner))
+            j = b + CLASSES * k
+            piece(o, j, 0, inner).wait_recv()
+            if k % 2 == 1:
+                go(piece(o, j, 0, side_peer))
+            go(piece(o, j, 2, inner))
+    for k in range(turns):
+        for o in outer:
+            piece(o, c + CLASSES * k, 0, inner).wait_recv()
+            go(piece(o, c + CLASSES * k, 2, inner))
+    other = flip1(s)
+    copy_to(cbuf, rowsout.at[other], send2.at[other, 0, 0], recv2.at[other, PIECES], inner).wait_recv()
+    for o in outer:
+        for j in range(PIECES):
+            piece(flip1(o), j, 0, inner).wait_recv()
+    for x in sends:
+        x.wait_send()
+    first("wait_send")
+
+    def drain(d, carry):
+        relay(d, "wait_send")
+        return carry
+
+    lax.fori_loop(1, length, drain, 0)
+    store.wait()
+    keep.wait()
+
+
+def exchange(sent, sel, param, inv, shards):
     reps = sel.shape[0]
+    rows, D = param.shape
     vmem = pl.BlockSpec(memory_space=pltpu.VMEM)
+    hbm = pl.BlockSpec(memory_space=pl.ANY)
     return pl.pallas_call(
-        functools.partial(sum_sent_kernel, reps),
+        functools.partial(exchange_kernel, reps, shards),
         out_shape=[
             jax.ShapeDtypeStruct((rows, D), jnp.float32),
-            jax.ShapeDtypeStruct((rows, BLK), jnp.float32),
+            jax.ShapeDtypeStruct((shards, rows, D), jnp.bfloat16),
         ],
-        in_specs=[vmem, vmem],
-        out_specs=[vmem, vmem],
+        in_specs=[vmem, vmem, hbm, vmem],
+        out_specs=[hbm, hbm],
         scratch_shapes=[
+            pltpu.VMEM((rows, D), jnp.float32),
+            pltpu.VMEM((rows, BLK), jnp.float32),
+            pltpu.VMEM((rows, D), jnp.float32),
+            pltpu.VMEM((rows, D), jnp.bfloat16),
             pltpu.VMEM((reps,) + sent.shape, sent.dtype),
             pltpu.SemaphoreType.DMA((reps, 3)),
             pltpu.SemaphoreType.DMA((reps,)),
+            pltpu.SemaphoreType.DMA((shards, PIECES, max(3, shards))),
+            pltpu.SemaphoreType.DMA((shards, PIECES + 1)),
+            pltpu.SemaphoreType.DMA((2,)),
         ],
         compiler_params=pltpu.CompilerParams(collective_id=0, has_side_effects=True),
-        name="sum_sent",
-    )(sent, sel)
-
-
-PIECES = 8
-
-
-def share_rows_kernel(shards, mine, out, send, recv, local):
-    dp, s = lax.axis_index("dp"), lax.axis_index("shard")
-    core, far = lax.rem(s, 2), s // 2
-    group = shards // 2
-    g = lax.rem(dp, 4)
-    flip1 = lambda v: v + 1 - 2 * lax.rem(v, 2)
-    flip2 = lambda v: v + 2 - 4 * lax.rem(v // 2, 2)
-    width = mine.shape[1] // PIECES
-    inner, side, deep = {"shard": flip1(s)}, {"dp": flip1(dp)}, {"dp": flip2(dp)}
-    outer = [2 * lax.rem(far + k, group) + core for k in range(1, group)]
-
-    barrier = pltpu.get_barrier_semaphore()
-    for peer in [inner, side, deep] + [{"shard": o} for o in outer]:
-        pl.semaphore_signal(barrier, inc=1, device_id=peer, device_id_type=MESH)
-    pl.semaphore_wait(barrier, 3 + len(outer))
-
-    lanes = lambda j: pl.ds(pl.multiple_of(j * width, BLK), width)
-
-    def piece(o, j, way, peer):
-        ref = out.at[o, :, lanes(j)]
-        return copy_to(ref, ref, send.at[o, j, way], recv.at[o, j], peer)
-
-    def own(j, k):
-        return copy_to(
-            mine.at[:, lanes(j)], out.at[s, :, lanes(j)], send.at[s, j, k], recv.at[s, j], {"shard": outer[k]}
-        )
-
-    sends = []
-
-    def go(c):
-        c.start()
-        sends.append(c)
-
-    for half in (0, 4):
-        for k in range(len(outer)):
-            go(own(g + half, k))
-    go(copy_to(mine, out.at[s], send.at[s, 0, group], recv.at[s, PIECES], inner))
-    keep = pltpu.make_async_copy(mine, out.at[s], local)
-    keep.start()
-
-    for half in (0, 4):
-        for o in outer:
-            j = g + half
-            piece(o, j, 0, inner).wait_recv()
-            go(piece(o, j, 0, side))
-            go(piece(o, j, 1, deep))
-            go(piece(o, j, 2, inner))
-    a, b, c = flip1(g), flip2(g), flip2(flip1(g))
-    for half in (0, 4):
-        for o in outer:
-            piece(o, a + half, 0, inner).wait_recv()
-            if half == 0:
-                go(piece(o, a + half, 1, deep))
-            go(piece(o, a + half, 2, inner))
-            piece(o, b + half, 0, inner).wait_recv()
-            if half == 4:
-                go(piece(o, b + half, 0, side))
-            go(piece(o, b + half, 2, inner))
-    for half in (0, 4):
-        for o in outer:
-            piece(o, c + half, 0, inner).wait_recv()
-            go(piece(o, c + half, 2, inner))
-    for o in outer:
-        for j in range(PIECES):
-            piece(flip1(o), j, 0, inner).wait_recv()
-    other = flip1(s)
-    copy_to(mine, out.at[other], send.at[other, 0, 0], recv.at[other, PIECES], inner).wait_recv()
-    for x in sends:
-        x.wait_send()
-    keep.wait()
-
-
-def share_rows(copy, shards):
-    rows, D = copy.shape
-    out = pl.pallas_call(
-        functools.partial(share_rows_kernel, shards),
-        out_shape=jax.ShapeDtypeStruct((shards, rows, D), copy.dtype),
-        in_specs=[pl.BlockSpec(memory_space=pltpu.VMEM)],
-        out_specs=pl.BlockSpec(memory_space=pl.ANY),
-        scratch_shapes=[
-            pltpu.SemaphoreType.DMA((shards, PIECES, max(3, shards))),
-            pltpu.SemaphoreType.DMA((shards, PIECES + 1)),
-            pltpu.SemaphoreType.DMA,
-        ],
-        compiler_params=pltpu.CompilerParams(collective_id=1, has_side_effects=True),
-        name="share_rows",
-    )(copy)
-    return out.reshape(shards * rows, D)
+        name="exchange",
+    )(sent, sel, param, inv)
 
 
 def on_device(grads, momentum, param, thresholds, sel_blocks, counts):
@@ -419,9 +420,9 @@
     new_momentum, sent = encode(
         momentum[0], grads[0], thresholds[None, :], sel_blocks, counts[:, 0], fwd, inv, width
     )
-    total, scale = sum_sent(sent, sel_blocks, rows, D)
-    new_param, copy = apply(total, scale, param, inv, width)
-    compute_copy = share_rows(copy, lax.axis_size("shard"))
+    shards = lax.axis_size("shard")
+    new_param, copies = exchange(sent, sel_blocks, param, inv, shards)
+    compute_copy = copies.reshape(shards * rows, D)
     return (new_momentum[None], new_param, compute_copy)
 
 

time: 87.2 us -> 75.4 us (0.86)
  Pallas kernels: 79.8 us -> 66.8 us
  local copies, waits for them, and re-layouts: 6.2 us -> 7.56 us
    pallas_call x3 -> x1, Pallas kernels: 67.8 us -> 54.8 us  [exchange(): pl.pallas_call(functools.partial(exchange_kernel, reps, shards), out_shap...]
    unnamed x1 -> x4, local copies, waits for them, and re-layouts: 6.2 us -> 7.56 us
where the time goes in v5:
time: 75.4 us; the launch traced here: 75.1 us
  Pallas kernels  66.8 us (89%)
  local copies, waits for them, and re-layouts  7.56 us (10%)
    pallas_call x1, Pallas kernels, exchange(): pl.pallas_call(functools.partial(exchange_kernel, reps, shards), out_shap...  54.8 us
    pallas_call x1, Pallas kernels, encode(): pl.pallas_call(functools.partial(encode_kernel, D // BLK), grid=(D // wid...  12 us
    unnamed x4, local copies, waits for them, and re-layouts  7.56 us

profile of v5, /device:TPU:0, one launch (start us, length us, event | category | flops | bytes accessed | tf_op | source)
XLA Modules:
  0.0 75.1 jit_solution(4616190326873067137)
XLA Ops:
  0.6 12.0 %encode.1 = (f32[96,8192]{1,0:T(8,128)}, bf16[768,128]{1,0:T(8,128)(2,1)}) custom-call(f32[96,8192]{1,0:T(8,128)} %bitcast.7, bf16[96,8192]{1,0:T(8,128)(2,1)} %bitcast.8, f32[1,96]{1,0:T(1,128)} %bitcast.9, s32[8,1,768]{2,1,0:T(1,128)} %sel.3, s32[8,1,768]{2,1,0:T(1,128)} %sel.3, s32[8]{0:T(128)} %bitcast.10, bf16[256,256]{1,0:T(8,128)(2,1)} %constant.4.clone.fwd, ...), custom_call_target="tpu_custom_call" | custom-call | tf_op jit(solution)/shard_map/encode/pallas_call | solution.py:105
  12.6 54.8 %exchange.1 = (f32[96,8192]{1,0:T(8,128)}, bf16[4,96,8192]{2,1,0:T(8,128)(2,1)}) custom-call(bf16[768,128]{1,0:T(8,128)(2,1)} %get-tuple-element.8.mine, s32[8,1,768]{2,1,0:T(1,128)} %sel.3, f32[96,8192]{1,0:T(8,128)} %param.15, bf16[256,256]{1,0:T(8,128)(2,1)} %constant.5.clone.inv), custom_call_target="tpu_custom_call" | custom-call | tf_op jit(solution)/shard_map/exchange/pallas_call | solution.py:391
  67.5 0.0 copy-start
  67.5 3.9 %copy.13 = f32[96,8192]{1,0:T(8,128)} copy(f32[96,8192]{1,0:T(8,128)} %get-tuple-element.15) | data formatting | bytes 6291456
  71.4 1.0 %copy-done = bf16[4,96,8192]{2,1,0:T(8,128)(2,1)S(1)} copy-done((bf16[4,96,8192]{2,1,0:T(8,128)(2,1)S(1)}, bf16[4,96,8192]{2,1,0:T(8,128)(2,1)}, u32[]{:S(2)}) %copy-start) | copy-done | bytes 6291480
  72.4 2.7 %copy.14 = bf16[384,8192]{1,0:T(8,128)(2,1)} copy(bf16[384,8192]{1,0:T(8,128)(2,1)S(1)} %bitcast.6) | data formatting | bytes 12582912
Async XLA Ops:
  67.5 4.9 %copy-start = (bf16[4,96,8192]{2,1,0:T(8,128)(2,1)S(1)}, bf16[4,96,8192]{2,1,0:T(8,128)(2,1)}, u32[]{:S(2)}) copy-start(bf16[4,96,8192]{2,1,0:T(8,128)(2,1)} %get-tuple-element.10) | copy-start | bytes 18874372

commit v6 on v5

--- a/solution.py
+++ b/solution.py
@@ -333,6 +333,7 @@
     for n in range(len(outer)):
         own(g + CLASSES * (turns - 1), n).start()
         sends.extend(own(g + CLASSES * k, n) for k in range(turns))
+    a, b, c = flip1(g), flip2(g), flip2(flip1(g))
     for k in range(turns):
         j = g + CLASSES * k
         for o in outer:
@@ -345,20 +346,23 @@
         if k == 1:
             store = pltpu.make_async_copy(pbuf, newparam, local.at[0])
             store.start()
+        if k == 2:
+            for direct in range(2, turns):
+                for n in range(len(outer)):
+                    go(own(c + CLASSES * direct, n))
     go(copy_to(cbuf, rowsout.at[s], send2.at[s, 0, group], recv2.at[s, PIECES], inner))
     keep = pltpu.make_async_copy(cbuf, rowsout.at[s], local.at[1])
     keep.start()
-    a, b, c = flip1(g), flip2(g), flip2(flip1(g))
     for k in range(turns):
         for o in outer:
             j = a + CLASSES * k
             piece(o, j, 0, inner).wait_recv()
-            if k % 2 == 0:
+            if k == 0:
                 go(piece(o, j, 1, deep))
             go(piece(o, j, 2, inner))
             j = b + CLASSES * k
             piece(o, j, 0, inner).wait_recv()
-            if k % 2 == 1:
+            if k == 1:
                 go(piece(o, j, 0, side_peer))
             go(piece(o, j, 2, inner))
     for k in range(turns):

time: 75.4 us -> 72.6 us (0.963)
  Pallas kernels: 66.8 us -> 64 us
    pallas_call x1, Pallas kernels: 54.8 us -> 52 us  [exchange(): pl.pallas_call(functools.partial(exchange_kernel, reps, shards), out_shap...]
where the time goes in v6:
time: 72.6 us; the launch traced here: 72.2 us
  Pallas kernels  64 us (88%)
  local copies, waits for them, and re-layouts  7.56 us (10%)
    pallas_call x1, Pallas kernels, exchange(): pl.pallas_call(functools.partial(exchange_kernel, reps, shards), out_shap...  52 us
    pallas_call x1, Pallas kernels, encode(): pl.pallas_call(functools.partial(encode_kernel, D // BLK), grid=(D // wid...  12 us
    unnamed x4, local copies, waits for them, and re-layouts  7.56 us

profile of v6, /device:TPU:0, one launch (start us, length us, event | category | flops | bytes accessed | tf_op | source)
XLA Modules:
  0.0 72.2 jit_solution(2424024550378218167)
XLA Ops:
  0.6 12.0 %encode.1 = (f32[96,8192]{1,0:T(8,128)}, bf16[768,128]{1,0:T(8,128)(2,1)}) custom-call(f32[96,8192]{1,0:T(8,128)} %bitcast.7, bf16[96,8192]{1,0:T(8,128)(2,1)} %bitcast.8, f32[1,96]{1,0:T(1,128)} %bitcast.9, s32[8,1,768]{2,1,0:T(1,128)} %sel.3, s32[8,1,768]{2,1,0:T(1,128)} %sel.3, s32[8]{0:T(128)} %bitcast.10, bf16[256,256]{1,0:T(8,128)(2,1)} %constant.4.clone.fwd, ...), custom_call_target="tpu_custom_call" | custom-call | tf_op jit(solution)/shard_map/encode/pallas_call | solution.py:105
  12.6 52.0 %exchange.1 = (f32[96,8192]{1,0:T(8,128)}, bf16[4,96,8192]{2,1,0:T(8,128)(2,1)}) custom-call(bf16[768,128]{1,0:T(8,128)(2,1)} %get-tuple-element.8.mine, s32[8,1,768]{2,1,0:T(1,128)} %sel.3, f32[96,8192]{1,0:T(8,128)} %param.15, bf16[256,256]{1,0:T(8,128)(2,1)} %constant.5.clone.inv), custom_call_target="tpu_custom_call" | custom-call | tf_op jit(solution)/shard_map/exchange/pallas_call | solution.py:395
  64.7 0.0 copy-start
  64.7 3.9 %copy.13 = f32[96,8192]{1,0:T(8,128)} copy(f32[96,8192]{1,0:T(8,128)} %get-tuple-element.15) | data formatting | bytes 6291456
  68.6 1.0 %copy-done = bf16[4,96,8192]{2,1,0:T(8,128)(2,1)S(1)} copy-done((bf16[4,96,8192]{2,1,0:T(8,128)(2,1)S(1)}, bf16[4,96,8192]{2,1,0:T(8,128)(2,1)}, u32[]{:S(2)}) %copy-start) | copy-done | bytes 6291480
  69.5 2.7 %copy.14 = bf16[384,8192]{1,0:T(8,128)(2,1)} copy(bf16[384,8192]{1,0:T(8,128)(2,1)S(1)} %bitcast.6) | data formatting | bytes 12582912
Async XLA Ops:
  64.7 4.9 %copy-start = (bf16[4,96,8192]{2,1,0:T(8,128)(2,1)S(1)}, bf16[4,96,8192]{2,1,0:T(8,128)(2,1)}, u32[]{:S(2)}) copy-start(bf16[4,96,8192]{2,1,0:T(8,128)(2,1)} %get-tuple-element.10) | copy-start | bytes 18874372
